TPU v7x, 32 devices: a whole 2x2x4 slice. The times are simulated.
32 devices in a mesh: groups: 2 (over x), ctx: 16 (over z, y, core).
Axes of the slice: x: 2, y: 2, z: 4, core: 2. Of those that a mesh axis runs over, the one named last changes fastest.
Arguments:
- ssm_input: bfloat16 [8192, 4096], P(('groups', 'ctx')), parts along dimension 0, may hold values from -18 to 18
- gate_input: bfloat16 [8192, 4096], P(('groups', 'ctx')), parts along dimension 0, may hold values from -6 to 6
- bc_input: bfloat16 [8192, 1024], P(('groups', 'ctx')), parts along dimension 0, may hold values from -6 to 6
- dt_raw: float32 [8192, 64], P(('groups', 'ctx')), parts along dimension 0, may hold values from -4 to 16
- offsets: int32 [38], P('groups'), parts along dimension 0, may hold values from 0 to 4096, as said below
- owners: int32 [36], P('groups'), parts along dimension 0, may hold values from 0 to 15, as said below
- conv_weight: float32 [4, 5120], replicated, may hold values from -3 to 3
- convolution_bias: float32 [5120], replicated, may hold values from -3 to 3
- a_log: float32 [64], replicated, may hold values from -3.6 to 2.5
- dt_bias: float32 [64], replicated, may hold values from -6.2 to -5.2
- d_skip: float32 [64], replicated, may hold values from 0.5 to 1.5
- norm_weight: float32 [4096], replicated, may hold values from 0.25 to 1.75
Outputs:
- gated_out: bfloat16 [8192, 4096], P(('groups', 'ctx')), parts along dimension 0
- decode_states: float32 [64, 64, 64, 128], P(('groups', 'ctx')), parts along dimension 0
There are 2 independent parts, one for each index of `groups`. A program takes and returns all parts, laid end to end along the dimension named above; an argument that names none is the same for every part. Nothing has to cross between parts.
Inputs may be any that keep to these rules, and one draw needn't show every extreme that they name: offsets[0] is 0, offsets[18] is 4096 and the offsets rise strictly; every document holds at most 512 tokens and one holds exactly 512; at most 4 documents end on the 256 tokens of one device, and exactly 4 on some device. `owners`: each device owns at most 2 documents, and some device exactly 2.
All inputs are finite; a program needn't handle non-finite values.
Results may differ from a plain program's by a relative error of at most 0.001.
The roundings to bfloat16 on the way count: a program that leaves them out, or rounds other values in their place, can miss the bound.
Values may be sent and summed in bfloat16 or wider, within the bound.
A program may use at most 128 MiB of HBM per device.

v0:
```python
import functools
import jax
import jax.numpy as jnp
from jax import lax
from jax.experimental import pallas as pl
from jax.experimental.pallas import tpu as pltpu
from jax.sharding import PartitionSpec as P

GROUP_HEADS = 16
KERNEL_WIDTH = 4
OWNER_SLOTS = 2
BLOCK_HEADS = 4
RIM = 8
VMEM_LIMIT = 48 * 1024 * 1024


def shifted(array, axis, by):
    devices = lax.axis_size(axis)
    pairs = [(i, i + by) for i in range(devices) if 0 <= i + by < devices]
    return lax.ppermute(array, axis, pairs)


def conv_silu(x, rim, mask, weight, bias):
    padded = jnp.concatenate([rim, x], 0).astype(jnp.float32)
    total = bias + weight[0:1] * (mask[:, 0:1] * pltpu.roll(padded, 3, 0)[RIM:])
    total = total + weight[1:2] * (mask[:, 1:2] * pltpu.roll(padded, 2, 0)[RIM:])
    total = total + weight[2:3] * (mask[:, 2:3] * pltpu.roll(padded, 1, 0)[RIM:])
    total = total + weight[3:4] * x.astype(jnp.float32)
    return (total / (1.0 + jnp.exp(-total))).astype(jnp.bfloat16)


def conv_kernel(groups, state_dim, x_ref, bc_ref, rim_x_ref, rim_bc_ref, mask_ref, wx_ref, bx_ref, wbc_ref,
                bbc_ref, end_ref, send_ref, c_ref, local_ref, b_scr):
    step = pl.program_id(0)
    width = x_ref.shape[1]
    length = x_ref.shape[0]
    mask = mask_ref[...]

    @pl.when(step == 0)
    def _():
        for part in range(2 * groups):
            cols = slice(part * state_dim, (part + 1) * state_dim)
            value = conv_silu(bc_ref[:, cols], rim_bc_ref[:, cols], mask, wbc_ref[:, cols], bbc_ref[:, cols])
            if part < groups:
                b_scr[part] = value
            else:
                c_ref[:, (part - groups) * state_dim:(part - groups + 1) * state_dim] = value

    xs = conv_silu(x_ref[...], rim_x_ref[...], mask, wx_ref[...], bx_ref[...])
    b_val = b_scr[step * groups // pl.num_programs(0)]
    send_ref[0, :, :width] = xs
    send_ref[0, :, width:] = b_val
    end = end_ref[0]
    heads = end.shape[0]
    x_t = xs.astype(jnp.float32).T.reshape(heads, width // heads, length)
    weighted = (x_t * end[:, None, :]).astype(jnp.bfloat16).reshape(width, length)
    local_ref[0] = jnp.dot(weighted, b_val, preferred_element_type=jnp.float32)


def state_kernel(docs, heads, offsets_ref, dest_ref, recv_ref, cd_ref, out_ref, carry_scr):
    block = pl.program_id(0)
    length = recv_ref.shape[1]
    width = out_ref.shape[1]
    state_dim = out_ref.shape[2]
    head_dim = width // heads

    @pl.when(block == 0)
    def _():
        out_ref[...] = jnp.zeros_like(out_ref)
        carry_scr[...] = jnp.zeros_like(carry_scr)

    first = block * length
    x_t = recv_ref[0, :, :width].astype(jnp.float32).T.reshape(heads, head_dim, length)
    b_val = recv_ref[0, :, width:]
    cum = cd_ref[0, :heads]
    dt = cd_ref[0, heads:]
    lane = lax.broadcasted_iota(jnp.int32, (heads, length), 1)
    incoming = carry_scr[...]

    def state_at(end, start):
        cum_end = jnp.sum(jnp.where(lane == end, cum, 0.0), axis=1, keepdims=True)
        covered = (lane >= start) & (lane <= end)
        weight = jnp.exp(jnp.where(covered, cum_end - cum, -jnp.inf)) * dt
        weighted = (x_t * weight[:, None, :]).astype(jnp.bfloat16).reshape(width, length)
        local = jnp.dot(weighted, b_val, preferred_element_type=jnp.float32)
        factor = jnp.where(start < 0, jnp.exp(cum_end), 0.0)
        return local + (factor[:, :, None] * incoming.reshape(heads, head_dim, state_dim)).reshape(width, state_dim)

    def visit(doc, last_start):
        start = offsets_ref[doc]
        end = offsets_ref[doc + 1] - 1

        @pl.when((end >= first) & (end < first + length))
        def _():
            out_ref[dest_ref[doc]] = state_at(end - first, start - first)

        return jnp.where(start < first + length, start, last_start)

    last_start = lax.fori_loop(0, docs, visit, jnp.int32(0))
    carry_scr[...] = state_at(jnp.int32(length - 1), last_start - first)


def main_kernel(send_ref, c_ref, cum_row_ref, cum_col_ref, cont_ref, dt_row_ref, start_ref, skip_ref, in_ref,
                gate_ref, norm_ref, out_ref, v_scr):
    blocks, length, total = send_ref.shape
    width = skip_ref.shape[1] // blocks
    heads = cum_row_ref.shape[0] // blocks
    head_dim = width // heads
    c_val = c_ref[...]
    contract = (((1,), (1,)), ((), ()))
    scores = lax.dot_general(c_val, send_ref[0, :, width:], contract, preferred_element_type=jnp.float32)
    row = lax.broadcasted_iota(jnp.int32, (length, length), 0)
    col = lax.broadcasted_iota(jnp.int32, (length, length), 1)
    causal = (col <= row) & (col >= start_ref[...])
    part = lax.broadcasted_iota(jnp.int32, (length, width), 1) // head_dim
    square = jnp.zeros((length, 1), jnp.float32)
    for block in range(blocks):
        xs = send_ref[block, :, :width]
        cols = slice(block * width, (block + 1) * width)
        weights, split = [], []
        cont = jnp.zeros((length, width), jnp.float32)
        for head in range(heads):
            at = block * heads + head
            gap = cum_col_ref[0, :, at:at + 1] - cum_row_ref[at:at + 1, :]
            decay = jnp.exp(jnp.where(causal, gap, -jnp.inf))
            weights.append((scores * decay * dt_row_ref[at:at + 1, :]).astype(jnp.bfloat16))
            split.append(jnp.where(part == head, xs, jnp.zeros_like(xs)))
            cont = jnp.where(part == head, cont_ref[0, :, at:at + 1], cont)
        intra = jnp.dot(jnp.concatenate(weights, 1), jnp.concatenate(split, 0), preferred_element_type=jnp.float32)
        state = in_ref[block]
        high = state.astype(jnp.bfloat16)
        low = (state - high.astype(jnp.float32)).astype(jnp.bfloat16)
        inter = lax.dot_general(c_val, high, contract, preferred_element_type=jnp.float32)
        inter = inter + lax.dot_general(c_val, low, contract, preferred_element_type=jnp.float32)
        y_sum = intra + inter * cont + skip_ref[:, cols] * xs.astype(jnp.float32)
        gate = gate_ref[:, cols].astype(jnp.float32)
        value = y_sum * (gate / (1.0 + jnp.exp(-gate)))
        v_scr[:, cols] = value
        square = square + jnp.sum(value * value, axis=1, keepdims=True)
    scale = lax.rsqrt(square / (blocks * width) + 1e-05)
    out_ref[...] = (v_scr[...] * scale * norm_ref[...]).astype(jnp.bfloat16)


def per_device(
    ssm_input,
    gate_input,
    bc_input,
    dt_raw,
    offsets,
    owners,
    conv_weight,
    convolution_bias,
    a_log,
    dt_bias,
    d_skip,
    norm_weight,
):
    length, inner_dim = ssm_input.shape
    heads = a_log.shape[0]
    head_dim = inner_dim // heads
    groups = heads // GROUP_HEADS
    state_dim = bc_input.shape[1] // (2 * groups)
    docs = offsets.shape[0] - 1
    devices = lax.axis_size("ctx")
    blocks = heads // BLOCK_HEADS
    width = BLOCK_HEADS * head_dim
    group_state = groups * state_dim
    channels = inner_dim + 2 * group_state
    base = lax.axis_index("ctx") * length

    tail = jnp.concatenate([ssm_input[length - RIM:], bc_input[length - RIM:]], 1)
    rim = shifted(tail, "ctx", 1)

    local_tok = jnp.arange(length, dtype=jnp.int32)
    tok_index = base + local_tok
    below = offsets[None, :] <= tok_index[:, None]
    doc_start = jnp.max(jnp.where(below, offsets[None, :], 0), 1)
    start_local = doc_start - base
    taps = jnp.arange(KERNEL_WIDTH, dtype=jnp.int32) - (KERNEL_WIDTH - 1)
    mask = jnp.where(local_tok[:, None] + taps[None, :] >= start_local[:, None], 1.0, 0.0).astype(jnp.float32)

    dt = jax.nn.softplus(dt_raw + dt_bias[None, :])
    cum = jnp.cumsum(-dt * jnp.exp(a_log)[None, :], axis=0)
    cum_rows = cum.T
    dt_rows = dt.T
    cum_last = cum_rows[:, length - 1:]
    end_weight = jnp.where(
        (local_tok >= start_local[length - 1])[None, :], jnp.exp(cum_last - cum_rows) * dt_rows, 0.0
    )
    through = jnp.where(start_local[length - 1] < 0, jnp.exp(cum_last), 0.0)
    cont = jnp.where((start_local < 0)[:, None], jnp.exp(cum), 0.0)

    device_heads = heads // devices
    cd_send = jnp.concatenate(
        [cum_rows.reshape(devices, device_heads, length), dt_rows.reshape(devices, device_heads, length)], 1
    )
    cd_recv = lax.all_to_all(cd_send, "ctx", split_axis=0, concat_axis=0, tiled=True)

    full = lambda shape: pl.BlockSpec(shape, lambda j: (0,) * len(shape))
    column = lambda rows: pl.BlockSpec((rows, width), lambda j: (0, j))
    send, c_proj, local_end = pl.pallas_call(
        functools.partial(conv_kernel, groups, state_dim),
        grid=(blocks,),
        in_specs=[
            column(length),
            full((length, 2 * group_state)),
            column(RIM),
            full((RIM, 2 * group_state)),
            full((length, KERNEL_WIDTH)),
            column(KERNEL_WIDTH),
            column(1),
            full((KERNEL_WIDTH, 2 * group_state)),
            full((1, 2 * group_state)),
            pl.BlockSpec((1, BLOCK_HEADS, length), lambda j: (j, 0, 0)),
        ],
        out_specs=[
            pl.BlockSpec((1, length, width + state_dim), lambda j: (j, 0, 0)),
            full((length, group_state)),
            pl.BlockSpec((1, width, state_dim), lambda j: (j, 0, 0)),
        ],
        out_shape=[
            jax.ShapeDtypeStruct((blocks, length, width + state_dim), jnp.bfloat16),
            jax.ShapeDtypeStruct((length, group_state), jnp.bfloat16),
            jax.ShapeDtypeStruct((blocks, width, state_dim), jnp.float32),
        ],
        scratch_shapes=[pltpu.VMEM((groups, length, state_dim), jnp.bfloat16)],
        compiler_params=pltpu.CompilerParams(vmem_limit_bytes=VMEM_LIMIT),
        name="conv",
    )(
        ssm_input,
        bc_input,
        rim[:, :inner_dim],
        rim[:, inner_dim:],
        mask,
        conv_weight[:, :inner_dim],
        convolution_bias[None, :inner_dim],
        conv_weight[:, inner_dim:],
        convolution_bias[None, inner_dim:],
        end_weight.reshape(blocks, BLOCK_HEADS, length),
    )

    device_width = inner_dim // devices
    if devices == blocks:
        outgoing = send
    else:
        share = devices // blocks
        x_part = send[:, :, :width].reshape(blocks, length, share, device_width)
        x_part = x_part.transpose(0, 2, 1, 3).reshape(devices, length, device_width)
        outgoing = jnp.concatenate([x_part, jnp.repeat(send[:, :, width:], share, axis=0)], 2)
    gathered = lax.all_to_all(outgoing, "ctx", split_axis=0, concat_axis=0, tiled=True)

    factor = jnp.repeat(through.reshape(heads), head_dim).reshape(blocks, width, 1)
    incoming = shifted(local_end, "ctx", 1)
    for _ in range(devices // 8 - 1):
        incoming = shifted(factor * incoming + local_end, "ctx", 1)

    doc_ids = jnp.arange(docs, dtype=jnp.int32)
    earlier = doc_ids[None, :] < doc_ids[:, None]
    owner_rank = jnp.sum(((owners[None, :] == owners[:, None]) & earlier).astype(jnp.int32), 1)
    dest_row = owners * OWNER_SLOTS + owner_rank
    rows = devices * OWNER_SLOTS
    states = pl.pallas_call(
        functools.partial(state_kernel, docs, device_heads),
        grid_spec=pltpu.PrefetchScalarGridSpec(
            num_scalar_prefetch=2,
            grid=(devices,),
            in_specs=[
                pl.BlockSpec((1, length, device_width + state_dim), lambda b, *_: (b, 0, 0)),
                pl.BlockSpec((1, 2 * device_heads, length), lambda b, *_: (b, 0, 0)),
            ],
            out_specs=pl.BlockSpec((rows, device_width, state_dim), lambda b, *_: (0, 0, 0)),
            scratch_shapes=[pltpu.VMEM((device_width, state_dim), jnp.float32)],
        ),
        out_shape=jax.ShapeDtypeStruct((rows, device_width, state_dim), jnp.float32),
        compiler_params=pltpu.CompilerParams(vmem_limit_bytes=VMEM_LIMIT),
        name="doc_states",
    )(offsets, dest_row, gathered, cd_recv)
    delivered = lax.all_to_all(
        states.reshape(devices, OWNER_SLOTS * device_width, state_dim), "ctx", split_axis=0, concat_axis=0, tiled=True
    )
    decode_states = (
        delivered.reshape(devices, OWNER_SLOTS, device_heads, head_dim, state_dim)
        .transpose(1, 0, 2, 3, 4)
        .reshape(OWNER_SLOTS, heads, head_dim, state_dim)
    )

    group_blocks = GROUP_HEADS // BLOCK_HEADS
    group_width = group_blocks * width
    per_group = lambda rows: pl.BlockSpec((rows, group_width), lambda g: (0, g))
    by_column = lambda a: a.reshape(length, groups, GROUP_HEADS).transpose(1, 0, 2)
    column_spec = pl.BlockSpec((1, length, GROUP_HEADS), lambda g: (g, 0, 0))
    row_spec = pl.BlockSpec((GROUP_HEADS, length), lambda g: (g, 0))
    gated_out = pl.pallas_call(
        main_kernel,
        grid=(groups,),
        in_specs=[
            pl.BlockSpec((group_blocks, length, width + state_dim), lambda g: (g, 0, 0)),
            pl.BlockSpec((length, state_dim), lambda g: (0, g)),
            row_spec,
            column_spec,
            column_spec,
            row_spec,
            pl.BlockSpec((length, 1), lambda g: (0, 0)),
            per_group(1),
            pl.BlockSpec((group_blocks, width, state_dim), lambda g: (g, 0, 0)),
            per_group(length),
            per_group(1),
        ],
        out_specs=per_group(length),
        out_shape=jax.ShapeDtypeStruct((length, inner_dim), jnp.bfloat16),
        scratch_shapes=[pltpu.VMEM((length, group_width), jnp.float32)],
        compiler_params=pltpu.CompilerParams(vmem_limit_bytes=VMEM_LIMIT),
        cost_estimate=pl.CostEstimate(flops=3_000_000_000, bytes_accessed=12_000_000, transcendentals=6_000_000),
        name="scan_gate_norm",
    )(
        send,
        c_proj,
        cum_rows,
        by_column(cum),
        by_column(cont),
        dt_rows,
        start_local[:, None],
        jnp.repeat(d_skip, head_dim)[None, :],
        incoming,
        gate_input,
        norm_weight[None, :],
    )
    return (gated_out, decode_states)


def solution(mesh):
    in_specs = (
        P(("groups", "ctx"), None),
        P(("groups", "ctx"), None),
        P(("groups", "ctx"), None),
        P(("groups", "ctx"), None),
        P("groups"),
        P("groups"),
        P(),
        P(),
        P(),
        P(),
        P(),
        P(),
    )
    out_specs = (P(("groups", "ctx"), None), P(("groups", "ctx"), None, None, None))
    return jax.shard_map(
        per_device, mesh=mesh, in_specs=in_specs, out_specs=out_specs, check_vma=False
    )
```

profile of v0, /device:TPU:18, one launch (start us, length us, event | category | flops | bytes accessed | tf_op | source)
XLA Modules:
  0.0 298.9 jit_solution(10753580781046510859)
XLA Ops:
  0.7 1.0 slice.37
  1.6 0.7 slice.38
  2.4 1.9 collective-permute-start
  4.3 0.7 exp.17
  5.0 1.0 copy_bitcast_fusion.1
  5.9 0.6 reduce-window.6
  6.9 0.7 select_reduce_fusion.1
  8.3 0.6 iota_compare_fusion.1
  9.8 1.0 multiply_select_fusion
  10.9 0.7 pad_maximum_fusion
  11.6 6.5 %all-to-all-start.1 = ((f32[16,8,256]{2,1,0:T(8,128)}), f32[16,8,256]{2,1,0:T(8,128)S(1)}, u32[]{:S(2)}, u32[]{:S(2)}) async-start(f32[16,8,256]{2,1,0:T(8,128)} %pad_maximum_fusion), calls=%async_computation.1 | async-start | bytes 262144 | tf_op jit(solution)/shard_map/all_to_all | solution.py:197
  18.2 0.8 slice.41.wx_ref
  19.0 0.7 slice.43.wbc_ref
  19.7 0.7 slice.42
  20.5 0.7 slice.44
  21.2 0.8 slice.49.rim_x_ref
  22.0 0.7 slice.50.rim_bc_ref
  22.8 9.9 %conv.1 = (bf16[16,256,384]{2,1,0:T(8,128)(2,1)}, bf16[256,512]{1,0:T(8,128)(2,1)S(1)}, f32[16,256,128]{2,1,0:T(8,128)S(1)}) custom-call(bf16[256,4096]{1,0:T(8,128)(2,1)S(1)} %copy-done, bf16[256,1024]{1,0:T(8,128)(2,1)S(1)} %copy-done.3, bf16[8,4096]{1,0:T(8,128)(2,1)S(1)} %slice.49.rim_x_ref, bf16[8,1024]{1,0:T(8,128)(2,1)S(1)} %slice.50.rim_bc_ref, ...), custom_call_target="tpu_custom_call" | custom-call | tf_op jit(solution)/shard_map/conv/pallas_call | solution.py:201
  32.7 1.3 copy-done.1
  34.0 0.7 copy-done.6
  34.7 6.2 %all-to-all-start = ((bf16[16,256,384]{2,1,0:T(8,128)(2,1)}), bf16[16,256,384]{2,1,0:T(8,128)(2,1)S(1)}, u32[]{:S(2)}, u32[]{:S(2)}) async-start(bf16[16,256,384]{2,1,0:T(8,128)(2,1)} %get-tuple-element.5.send_ref), calls=%async_computation | async-start | bytes 6291456 | tf_op jit(solution)/shard_map/all_to_all | solution.py:250
  41.1 69.9 %all-to-all-done.recv_ref = bf16[16,256,384]{2,1,0:T(8,128)(2,1)S(1)} async-done(((bf16[16,256,384]{2,1,0:T(8,128)(2,1)}), bf16[16,256,384]{2,1,0:T(8,128)(2,1)S(1)}, u32[]{:S(2)}, u32[]{:S(2)}) %all-to-all-start) | async-done | bytes 3145760 | tf_op jit(solution)/shard_map/all_to_all | solution.py:250
  111.0 17.1 %doc_states.1 = f32[32,256,128]{2,1,0:T(8,128)} custom-call(s32[19]{0:T(128)S(1)} %copy-done.4, s32[18]{0:T(128)S(1)} %multiply_add_fusion.1.dest_ref, bf16[16,256,384]{2,1,0:T(8,128)(2,1)S(1)} %all-to-all-done.recv_ref, f32[16,8,256]{2,1,0:T(8,128)S(1)} %all-to-all-done.1.cd_ref), custom_call_target="tpu_custom_call" | custom-call | tf_op jit(solution)/shard_map/doc_states/pallas_call | solution.py:262
  128.1 4.8 %all-to-all-start.2 = ((f32[16,512,128]{2,1,0:T(8,128)}), f32[16,512,128]{2,1,0:T(8,128)}, u32[]{:S(2)}, u32[]{:S(2)}) async-start(f32[16,512,128]{2,1,0:T(8,128)} %bitcast.45), calls=%async_computation.2 | async-start | bytes 8388608 | tf_op jit(solution)/shard_map/all_to_all | solution.py:278
  132.9 2.1 collective-permute-start.1
  135.2 112.9 %collective-permute-done.1 = f32[16,256,128]{2,1,0:T(8,128)} collective-permute-done((f32[16,256,128]{2,1,0:T(8,128)S(1)}, f32[16,256,128]{2,1,0:T(8,128)}, u32[]{:S(2)}, u32[]{:S(2)}) %collective-permute-start.1) | collective-permute-done | bytes 2097184 | tf_op jit(solution)/shard_map/ppermute | solution.py:20
  248.1 2.9 multiply_add_fusion
  251.0 1.9 collective-permute-start.2
  253.7 25.8 %collective-permute-done.2.in_ref = f32[16,256,128]{2,1,0:T(8,128)} collective-permute-done((f32[16,256,128]{2,1,0:T(8,128)}, f32[16,256,128]{2,1,0:T(8,128)}, u32[]{:S(2)}, u32[]{:S(2)}) %collective-permute-start.2) | collective-permute-done | bytes 2097184 | tf_op jit(solution)/shard_map/ppermute | solution.py:20
  279.6 1.6 copy-done.5
  281.1 12.9 %scan_gate_norm.1 = bf16[256,4096]{1,0:T(8,128)(2,1)} custom-call(bf16[16,256,384]{2,1,0:T(8,128)(2,1)} %get-tuple-element.5.send_ref, bf16[256,512]{1,0:T(8,128)(2,1)S(1)} %copy-done.7, f32[64,256]{1,0:T(8,128)S(1)} %copy_bitcast_fusion.cum_row_ref, f32[4,256,16]{2,1,0:T(8,128)S(1)} %bitcast.40, f32[4,256,16]{2,1,0:T(8,128)S(1)} %bitcast.39, ...), custom_call_target="tpu_custom_call" | custom-call | flops 3000000000 | bytes 12000000 | tf_op jit(solution)/shard_map/scan_gate_norm/pallas_call | solution.py:293
  294.1 4.8 %copy.33 = f32[16,2,4,64,128]{4,3,2,0,1:T(8,128)} copy(f32[16,2,4,64,128]{4,3,2,1,0:T(8,128)} %bitcast.13) | data formatting | bytes 8388608 | tf_op jit(solution)/shard_map/reshape | solution.py:282
  (49 shorter events, 2.7 us)
Async XLA Ops:
  0.6 22.1 %copy-start = (bf16[256,4096]{1,0:T(8,128)(2,1)S(1)}, bf16[256,4096]{1,0:T(8,128)(2,1)}, u32[]{:S(2)}) copy-start(bf16[256,4096]{1,0:T(8,128)(2,1)} %x_ref.1) | copy-start | bytes 6291460
  0.6 22.1 %copy-start.3 = (bf16[256,1024]{1,0:T(8,128)(2,1)S(1)}, bf16[256,1024]{1,0:T(8,128)(2,1)}, u32[]{:S(2)}) copy-start(bf16[256,1024]{1,0:T(8,128)(2,1)} %bc_ref.1) | copy-start | bytes 1572868
  2.4 18.8 %collective-permute-start = (bf16[8,5120]{1,0:T(8,128)(2,1)S(1)}, bf16[8,5120]{1,0:T(8,128)(2,1)}, u32[]{:S(2)}, u32[]{:S(2)}) collective-permute-start(bf16[8,5120]{1,0:T(8,128)(2,1)S(1)} %pad_maximum_fusion.1), channel_id=1, source_target_pairs={{0,1},{1,2},{2,3},{3,4},{4,5},{5,6},{6,7},{7,8},{8,9},{9,10},{10,1... | collective-permute-start | bytes 245768 | tf_op jit(solution)/shard_map/ppermute | solution.py:20
  11.6 23.1 %all-to-all-start.1 = ((f32[16,8,256]{2,1,0:T(8,128)}), f32[16,8,256]{2,1,0:T(8,128)S(1)}, u32[]{:S(2)}, u32[]{:S(2)}) async-start(f32[16,8,256]{2,1,0:T(8,128)} %pad_maximum_fusion), calls=%async_computation.1 | async-start | bytes 262144 | tf_op jit(solution)/shard_map/all_to_all | solution.py:197
  32.7 1.3 copy-start.1
  34.0 0.7 copy-start.6
  34.7 6.2 %copy-start.10 = (s32[18]{0:T(128)S(1)}, s32[18]{0:T(128)}, u32[]{:S(2)}) copy-start(s32[18]{0:T(128)} %param.17) | copy-start | bytes 220
  34.7 76.3 %copy-start.4 = (s32[19]{0:T(128)S(1)}, s32[19]{0:T(128)}, u32[]{:S(2)}) copy-start(s32[19]{0:T(128)} %offsets_ref.1) | copy-start | bytes 232
  34.7 76.3 %all-to-all-start = ((bf16[16,256,384]{2,1,0:T(8,128)(2,1)}), bf16[16,256,384]{2,1,0:T(8,128)(2,1)S(1)}, u32[]{:S(2)}, u32[]{:S(2)}) async-start(bf16[16,256,384]{2,1,0:T(8,128)(2,1)} %get-tuple-element.5.send_ref), calls=%async_computation | async-start | bytes 6291456 | tf_op jit(solution)/shard_map/all_to_all | solution.py:250
  128.1 4.8 %copy-start.2 = (f32[16,256,128]{2,1,0:T(8,128)S(1)}, f32[16,256,128]{2,1,0:T(8,128)}, u32[]{:S(2)}) copy-start(f32[16,256,128]{2,1,0:T(8,128)} %copy-done.1) | copy-start | bytes 6291460
  128.1 166.0 %all-to-all-start.2 = ((f32[16,512,128]{2,1,0:T(8,128)}), f32[16,512,128]{2,1,0:T(8,128)}, u32[]{:S(2)}, u32[]{:S(2)}) async-start(f32[16,512,128]{2,1,0:T(8,128)} %bitcast.45), calls=%async_computation.2 | async-start | bytes 8388608 | tf_op jit(solution)/shard_map/all_to_all | solution.py:278
  132.9 115.2 %collective-permute-start.1 = (f32[16,256,128]{2,1,0:T(8,128)S(1)}, f32[16,256,128]{2,1,0:T(8,128)}, u32[]{:S(2)}, u32[]{:S(2)}) collective-permute-start(f32[16,256,128]{2,1,0:T(8,128)S(1)} %copy-done.2), channel_id=1, source_target_pairs={{0,1},{1,2},{2,3},{3,4},{4,5},{5,6},{6,7},{7,8},{8,9},{9,10},{10,1... | collective-permute-start | bytes 6291464 | tf_op jit(solution)/shard_map/ppermute | solution.py:20
  135.2 118.3 %copy-start.9 = (f32[64]{0:T(128)S(1)}, f32[64]{0:T(128)}, u32[]{:S(2)}) copy-start(f32[64]{0:T(128)} %param.22) | copy-start | bytes 772
  135.2 144.3 %copy-start.7 = (bf16[256,512]{1,0:T(8,128)(2,1)S(1)}, bf16[256,512]{1,0:T(8,128)(2,1)}, u32[]{:S(2)}) copy-start(bf16[256,512]{1,0:T(8,128)(2,1)} %copy-done.6) | copy-start | bytes 786436
  135.2 144.3 %copy-start.8 = (f32[4096]{0:T(1024)S(1)}, f32[4096]{0:T(1024)}, u32[]{:S(2)}) copy-start(f32[4096]{0:T(1024)} %param.23) | copy-start | bytes 49156
  251.0 28.6 %collective-permute-start.2 = (f32[16,256,128]{2,1,0:T(8,128)}, f32[16,256,128]{2,1,0:T(8,128)}, u32[]{:S(2)}, u32[]{:S(2)}) collective-permute-start(f32[16,256,128]{2,1,0:T(8,128)} %multiply_add_fusion), channel_id=1, source_target_pairs={{0,1},{1,2},{2,3},{3,4},{4,5},{5,6},{6,7},{7,8},{8,9},{9,10},{10,1... | collective-permute-start | bytes 6291464 | tf_op jit(solution)/shard_map/ppermute | solution.py:20
  279.6 1.6 copy-start.5
where the time goes:
time: 300 us; the launch traced here: 299 us
  waiting for transfers between devices  209 us (70%)
  Pallas kernels  40 us (13%)
  starting transfers between devices  23.3 us (8%)
  local copies, waits for them, and re-layouts  17.2 us (6%)
  other arithmetic  8.29 us (3%)
    ppermute x3, waiting for transfers between devices, shifted(): return lax.ppermute(array, axis, pairs)  139 us
    all_to_all x1, waiting for transfers between devices, per_device(): lax.all_to_all(outgoing, 'ctx', split_axis=0, concat_axis=0, tiled=True)  69.9 us
    pallas_call x1, Pallas kernels, per_device(): pl.pallas_call(functools.partial(state_kernel, docs, device_heads), grid_...  17.1 us
    pallas_call x1, Pallas kernels, per_device(): pl.pallas_call(main_kernel, grid=(groups,), in_specs=[pl.BlockSpec((group...  12.9 us
    pallas_call x1, Pallas kernels, per_device(): pl.pallas_call(functools.partial(conv_kernel, groups, state_dim), grid=(b...  9.94 us
    all_to_all x1, starting transfers between devices, per_device(): lax.all_to_all(cd_send, 'ctx', split_axis=0, concat_axis=0, tiled=True)  6.46 us
    all_to_all x1, starting transfers between devices, per_device(): lax.all_to_all(outgoing, 'ctx', split_axis=0, concat_axis=0, tiled=True)  6.15 us
  transfers between devices with their start and end apart: 6, of which 3 were waited for; matrix products, arithmetic and copies ran while one was open for 5% of the time, Pallas kernels for 8%

commit v1 on v0

--- a/solution.py
+++ b/solution.py
@@ -1,4 +1,5 @@
 import functools
+import math
 import jax
 import jax.numpy as jnp
 from jax import lax
@@ -11,6 +12,9 @@
 OWNER_SLOTS = 2
 BLOCK_HEADS = 4
 RIM = 8
+SCALE_ROWS = 16
+LEVELS = 8.0
+CODE_MAX = 32767.0
 VMEM_LIMIT = 48 * 1024 * 1024
 
 
@@ -18,6 +22,26 @@
     devices = lax.axis_size(axis)
     pairs = [(i, i + by) for i in range(devices) if 0 <= i + by < devices]
     return lax.ppermute(array, axis, pairs)
+
+
+def encode(value):
+    rows, lanes = value.shape
+    parts = value.reshape(rows // SCALE_ROWS, SCALE_ROWS, lanes)
+    top = jnp.max(jnp.abs(parts), axis=1)
+    level = jnp.ceil(jnp.log(jnp.maximum(top, 1e-30)) * (LEVELS / math.log(2.0)))
+    unit = jnp.exp2(level * (-1.0 / LEVELS)) * CODE_MAX
+    coded = jnp.clip(jnp.round(parts * unit[:, None, :]), -CODE_MAX, CODE_MAX).reshape(rows, lanes)
+    if level.shape[0] < SCALE_ROWS:
+        level = jnp.concatenate([level, jnp.zeros((SCALE_ROWS - level.shape[0], lanes), jnp.float32)], 0)
+    return coded.astype(jnp.int32).astype(jnp.int16), level.astype(jnp.int32).astype(jnp.int16)
+
+
+def decode(coded, level):
+    rows, lanes = coded.shape
+    unit = jnp.exp2(level.astype(jnp.int32).astype(jnp.float32) * (1.0 / LEVELS)) * (1.0 / CODE_MAX)
+    unit = unit[:rows // SCALE_ROWS]
+    parts = coded.astype(jnp.int32).astype(jnp.float32).reshape(rows // SCALE_ROWS, SCALE_ROWS, lanes)
+    return (parts * unit[:, None, :]).reshape(rows, lanes)
 
 
 def conv_silu(x, rim, mask, weight, bias):
@@ -30,7 +54,7 @@
 
 
 def conv_kernel(groups, state_dim, x_ref, bc_ref, rim_x_ref, rim_bc_ref, mask_ref, wx_ref, bx_ref, wbc_ref,
-                bbc_ref, end_ref, send_ref, c_ref, local_ref, b_scr):
+                bbc_ref, end_ref, send_ref, c_ref, local_ref, code_ref, b_scr):
     step = pl.program_id(0)
     width = x_ref.shape[1]
     length = x_ref.shape[0]
@@ -54,28 +78,48 @@
     heads = end.shape[0]
     x_t = xs.astype(jnp.float32).T.reshape(heads, width // heads, length)
     weighted = (x_t * end[:, None, :]).astype(jnp.bfloat16).reshape(width, length)
-    local_ref[0] = jnp.dot(weighted, b_val, preferred_element_type=jnp.float32)
-
-
-def state_kernel(docs, heads, offsets_ref, dest_ref, recv_ref, cd_ref, out_ref, carry_scr):
+    local = jnp.dot(weighted, b_val, preferred_element_type=jnp.float32)
+    local_ref[0] = local
+    code_ref[0, :width], code_ref[0, width:] = encode(local)
+
+
+def relay_kernel(code_ref, local_ref, factor_ref, out_ref):
+    width = local_ref.shape[1]
+    value = factor_ref[0] * decode(code_ref[0, :width], code_ref[0, width:]) + local_ref[0]
+    out_ref[0, :width], out_ref[0, width:] = encode(value)
+
+
+def deliver_kernel(code_ref, out_ref):
+    slots, heads, head_dim, state_dim = out_ref.shape
+    width = heads * head_dim
+    for slot in range(slots):
+        value = decode(code_ref[0, slot, :width], code_ref[0, slot, width:])
+        out_ref[slot] = value.reshape(heads, head_dim, state_dim)
+
+
+def state_kernel(docs, heads, offsets_ref, dest_ref, recv_ref, cd_ref, mask_ref, weight_ref, bias_ref, out_ref,
+                 carry_scr, rim_scr):
     block = pl.program_id(0)
     length = recv_ref.shape[1]
-    width = out_ref.shape[1]
     state_dim = out_ref.shape[2]
+    width = out_ref.shape[1] - SCALE_ROWS
     head_dim = width // heads
 
     @pl.when(block == 0)
     def _():
         out_ref[...] = jnp.zeros_like(out_ref)
         carry_scr[...] = jnp.zeros_like(carry_scr)
+        rim_scr[...] = jnp.zeros_like(rim_scr)
 
     first = block * length
-    x_t = recv_ref[0, :, :width].astype(jnp.float32).T.reshape(heads, head_dim, length)
-    b_val = recv_ref[0, :, width:]
+    raw = recv_ref[0]
+    conv = conv_silu(raw, rim_scr[...], mask_ref[...], weight_ref[...], bias_ref[...])
+    rim_scr[...] = raw[length - RIM:]
+    x_t = conv[:, :width].astype(jnp.float32).T.reshape(heads, head_dim, length)
+    b_val = conv[:, width:]
     cum = cd_ref[0, :heads]
     dt = cd_ref[0, heads:]
     lane = lax.broadcasted_iota(jnp.int32, (heads, length), 1)
-    incoming = carry_scr[...]
 
     def state_at(end, start):
         cum_end = jnp.sum(jnp.where(lane == end, cum, 0.0), axis=1, keepdims=True)
@@ -84,7 +128,8 @@
         weighted = (x_t * weight[:, None, :]).astype(jnp.bfloat16).reshape(width, length)
         local = jnp.dot(weighted, b_val, preferred_element_type=jnp.float32)
         factor = jnp.where(start < 0, jnp.exp(cum_end), 0.0)
-        return local + (factor[:, :, None] * incoming.reshape(heads, head_dim, state_dim)).reshape(width, state_dim)
+        carried = factor[:, :, None] * carry_scr[...].reshape(heads, head_dim, state_dim)
+        return local + carried.reshape(width, state_dim)
 
     def visit(doc, last_start):
         start = offsets_ref[doc]
@@ -92,7 +137,8 @@
 
         @pl.when((end >= first) & (end < first + length))
         def _():
-            out_ref[dest_ref[doc]] = state_at(end - first, start - first)
+            row = dest_ref[doc]
+            out_ref[row, :width], out_ref[row, width:] = encode(state_at(end - first, start - first))
 
         return jnp.where(start < first + length, start, last_start)
 
@@ -127,7 +173,7 @@
             split.append(jnp.where(part == head, xs, jnp.zeros_like(xs)))
             cont = jnp.where(part == head, cont_ref[0, :, at:at + 1], cont)
         intra = jnp.dot(jnp.concatenate(weights, 1), jnp.concatenate(split, 0), preferred_element_type=jnp.float32)
-        state = in_ref[block]
+        state = decode(in_ref[block, :width], in_ref[block, width:])
         high = state.astype(jnp.bfloat16)
         low = (state - high.astype(jnp.float32)).astype(jnp.bfloat16)
         inter = lax.dot_general(c_val, high, contract, preferred_element_type=jnp.float32)
@@ -168,16 +214,31 @@
     channels = inner_dim + 2 * group_state
     base = lax.axis_index("ctx") * length
 
+    device_width = inner_dim // devices
+    device_heads = heads // devices
+    b_raw = bc_input[:, :group_state].reshape(length, groups, state_dim)
+    outgoing = jnp.concatenate(
+        [ssm_input.reshape(length, devices, device_width), jnp.repeat(b_raw, devices // groups, axis=1)], 2
+    ).transpose(1, 0, 2)
+    gathered = lax.all_to_all(outgoing, "ctx", split_axis=0, concat_axis=0, tiled=True)
+
     tail = jnp.concatenate([ssm_input[length - RIM:], bc_input[length - RIM:]], 1)
     rim = shifted(tail, "ctx", 1)
 
     local_tok = jnp.arange(length, dtype=jnp.int32)
-    tok_index = base + local_tok
-    below = offsets[None, :] <= tok_index[:, None]
-    doc_start = jnp.max(jnp.where(below, offsets[None, :], 0), 1)
-    start_local = doc_start - base
     taps = jnp.arange(KERNEL_WIDTH, dtype=jnp.int32) - (KERNEL_WIDTH - 1)
-    mask = jnp.where(local_tok[:, None] + taps[None, :] >= start_local[:, None], 1.0, 0.0).astype(jnp.float32)
+
+    def start_of(tokens):
+        below = offsets[None, :] <= tokens[:, None]
+        return jnp.max(jnp.where(below, offsets[None, :], 0), 1)
+
+    def tap_mask(tokens, starts):
+        return jnp.where(tokens[:, None] + taps[None, :] >= starts[:, None], 1.0, 0.0).astype(jnp.float32)
+
+    start_local = start_of(base + local_tok) - base
+    mask = tap_mask(local_tok, start_local)
+    all_tok = jnp.arange(devices * length, dtype=jnp.int32)
+    all_mask = tap_mask(all_tok, start_of(all_tok))
 
     dt = jax.nn.softplus(dt_raw + dt_bias[None, :])
     cum = jnp.cumsum(-dt * jnp.exp(a_log)[None, :], axis=0)
@@ -190,38 +251,43 @@
     through = jnp.where(start_local[length - 1] < 0, jnp.exp(cum_last), 0.0)
     cont = jnp.where((start_local < 0)[:, None], jnp.exp(cum), 0.0)
 
-    device_heads = heads // devices
     cd_send = jnp.concatenate(
         [cum_rows.reshape(devices, device_heads, length), dt_rows.reshape(devices, device_heads, length)], 1
     )
     cd_recv = lax.all_to_all(cd_send, "ctx", split_axis=0, concat_axis=0, tiled=True)
 
+    code_spec = pl.BlockSpec((1, width + SCALE_ROWS, state_dim), lambda j: (j, 0, 0))
+    code_shape = jax.ShapeDtypeStruct((blocks, width + SCALE_ROWS, state_dim), jnp.int16)
+    bias_row = convolution_bias[None, :]
     full = lambda shape: pl.BlockSpec(shape, lambda j: (0,) * len(shape))
+    after_x = lambda rows: pl.BlockSpec((rows, 2 * group_state), lambda j: (0, inner_dim // (2 * group_state)))
     column = lambda rows: pl.BlockSpec((rows, width), lambda j: (0, j))
-    send, c_proj, local_end = pl.pallas_call(
+    send, c_proj, local_end, local_code = pl.pallas_call(
         functools.partial(conv_kernel, groups, state_dim),
         grid=(blocks,),
         in_specs=[
             column(length),
             full((length, 2 * group_state)),
             column(RIM),
-            full((RIM, 2 * group_state)),
+            after_x(RIM),
             full((length, KERNEL_WIDTH)),
             column(KERNEL_WIDTH),
             column(1),
-            full((KERNEL_WIDTH, 2 * group_state)),
-            full((1, 2 * group_state)),
+            after_x(KERNEL_WIDTH),
+            after_x(1),
             pl.BlockSpec((1, BLOCK_HEADS, length), lambda j: (j, 0, 0)),
         ],
         out_specs=[
             pl.BlockSpec((1, length, width + state_dim), lambda j: (j, 0, 0)),
             full((length, group_state)),
             pl.BlockSpec((1, width, state_dim), lambda j: (j, 0, 0)),
+            code_spec,
         ],
         out_shape=[
             jax.ShapeDtypeStruct((blocks, length, width + state_dim), jnp.bfloat16),
             jax.ShapeDtypeStruct((length, group_state), jnp.bfloat16),
             jax.ShapeDtypeStruct((blocks, width, state_dim), jnp.float32),
+            code_shape,
         ],
         scratch_shapes=[pltpu.VMEM((groups, length, state_dim), jnp.bfloat16)],
         compiler_params=pltpu.CompilerParams(vmem_limit_bytes=VMEM_LIMIT),
@@ -229,36 +295,51 @@
     )(
         ssm_input,
         bc_input,
-        rim[:, :inner_dim],
-        rim[:, inner_dim:],
+        rim,
+        rim,
         mask,
-        conv_weight[:, :inner_dim],
-        convolution_bias[None, :inner_dim],
-        conv_weight[:, inner_dim:],
-        convolution_bias[None, inner_dim:],
+        conv_weight,
+        bias_row,
+        conv_weight,
+        bias_row,
         end_weight.reshape(blocks, BLOCK_HEADS, length),
     )
 
-    device_width = inner_dim // devices
-    if devices == blocks:
-        outgoing = send
-    else:
-        share = devices // blocks
-        x_part = send[:, :, :width].reshape(blocks, length, share, device_width)
-        x_part = x_part.transpose(0, 2, 1, 3).reshape(devices, length, device_width)
-        outgoing = jnp.concatenate([x_part, jnp.repeat(send[:, :, width:], share, axis=0)], 2)
-    gathered = lax.all_to_all(outgoing, "ctx", split_axis=0, concat_axis=0, tiled=True)
-
     factor = jnp.repeat(through.reshape(heads), head_dim).reshape(blocks, width, 1)
-    incoming = shifted(local_end, "ctx", 1)
+    incoming = shifted(local_code, "ctx", 1)
     for _ in range(devices // 8 - 1):
-        incoming = shifted(factor * incoming + local_end, "ctx", 1)
+        relayed = pl.pallas_call(
+            relay_kernel,
+            grid=(blocks,),
+            in_specs=[
+                code_spec,
+                pl.BlockSpec((1, width, state_dim), lambda j: (j, 0, 0)),
+                pl.BlockSpec((1, width, 1), lambda j: (j, 0, 0)),
+            ],
+            out_specs=code_spec,
+            out_shape=code_shape,
+            name="relay",
+        )(incoming, local_end, factor)
+        incoming = shifted(relayed, "ctx", 1)
+    gathered, incoming = lax.optimization_barrier((gathered, incoming))
+
+    mine = lax.axis_index("ctx")
+    b_first = inner_dim + (mine * groups // devices) * state_dim
+    taps_and_bias = jnp.concatenate([conv_weight, bias_row], 0)
+    own_taps = jnp.concatenate(
+        [
+            lax.dynamic_slice_in_dim(taps_and_bias, mine * device_width, device_width, 1),
+            lax.dynamic_slice_in_dim(taps_and_bias, b_first, state_dim, 1),
+        ],
+        1,
+    )
 
     doc_ids = jnp.arange(docs, dtype=jnp.int32)
     earlier = doc_ids[None, :] < doc_ids[:, None]
     owner_rank = jnp.sum(((owners[None, :] == owners[:, None]) & earlier).astype(jnp.int32), 1)
     dest_row = owners * OWNER_SLOTS + owner_rank
     rows = devices * OWNER_SLOTS
+    code_rows = device_width + SCALE_ROWS
     states = pl.pallas_call(
         functools.partial(state_kernel, docs, device_heads),
         grid_spec=pltpu.PrefetchScalarGridSpec(
@@ -267,22 +348,31 @@
             in_specs=[
                 pl.BlockSpec((1, length, device_width + state_dim), lambda b, *_: (b, 0, 0)),
                 pl.BlockSpec((1, 2 * device_heads, length), lambda b, *_: (b, 0, 0)),
+                pl.BlockSpec((length, KERNEL_WIDTH), lambda b, *_: (b, 0)),
+                pl.BlockSpec((KERNEL_WIDTH, device_width + state_dim), lambda b, *_: (0, 0)),
+                pl.BlockSpec((1, device_width + state_dim), lambda b, *_: (0, 0)),
             ],
-            out_specs=pl.BlockSpec((rows, device_width, state_dim), lambda b, *_: (0, 0, 0)),
-            scratch_shapes=[pltpu.VMEM((device_width, state_dim), jnp.float32)],
+            out_specs=pl.BlockSpec((rows, code_rows, state_dim), lambda b, *_: (0, 0, 0)),
+            scratch_shapes=[
+                pltpu.VMEM((device_width, state_dim), jnp.float32),
+                pltpu.VMEM((RIM, device_width + state_dim), jnp.bfloat16),
+            ],
         ),
-        out_shape=jax.ShapeDtypeStruct((rows, device_width, state_dim), jnp.float32),
+        out_shape=jax.ShapeDtypeStruct((rows, code_rows, state_dim), jnp.int16),
         compiler_params=pltpu.CompilerParams(vmem_limit_bytes=VMEM_LIMIT),
         name="doc_states",
-    )(offsets, dest_row, gathered, cd_recv)
+    )(offsets, dest_row, gathered, cd_recv, all_mask, own_taps[:KERNEL_WIDTH], own_taps[KERNEL_WIDTH:])
     delivered = lax.all_to_all(
-        states.reshape(devices, OWNER_SLOTS * device_width, state_dim), "ctx", split_axis=0, concat_axis=0, tiled=True
-    )
-    decode_states = (
-        delivered.reshape(devices, OWNER_SLOTS, device_heads, head_dim, state_dim)
-        .transpose(1, 0, 2, 3, 4)
-        .reshape(OWNER_SLOTS, heads, head_dim, state_dim)
-    )
+        states.reshape(devices, OWNER_SLOTS * code_rows, state_dim), "ctx", split_axis=0, concat_axis=0, tiled=True
+    )
+    decode_states = pl.pallas_call(
+        deliver_kernel,
+        grid=(devices,),
+        in_specs=[pl.BlockSpec((1, OWNER_SLOTS, code_rows, state_dim), lambda j: (j, 0, 0, 0))],
+        out_specs=pl.BlockSpec((OWNER_SLOTS, device_heads, head_dim, state_dim), lambda j: (0, j, 0, 0)),
+        out_shape=jax.ShapeDtypeStruct((OWNER_SLOTS, heads, head_dim, state_dim), jnp.float32),
+        name="deliver",
+    )(delivered.reshape(devices, OWNER_SLOTS, code_rows, state_dim))
 
     group_blocks = GROUP_HEADS // BLOCK_HEADS
     group_width = group_blocks * width
@@ -302,7 +392,7 @@
             row_spec,
             pl.BlockSpec((length, 1), lambda g: (0, 0)),
             per_group(1),
-            pl.BlockSpec((group_blocks, width, state_dim), lambda g: (g, 0, 0)),
+            pl.BlockSpec((group_blocks, width + SCALE_ROWS, state_dim), lambda g: (g, 0, 0)),
             per_group(length),
             per_group(1),
         ],

time: 300 us -> 245 us (0.82)
  waiting for transfers between devices: 209 us -> 124 us
  Pallas kernels: 40 us -> 71.9 us
    all_to_all x1, waiting for transfers between devices: 69.9 us -> 0.01 us  [per_device(): lax.all_to_all(outgoing, 'ctx', split_axis=0, concat_axis=0, tiled=True)]
    ppermute x3, waiting for transfers between devices: 139 us -> 88.2 us  [shifted(): return lax.ppermute(array, axis, pairs)]
    all_to_all x1, waiting for transfers between devices: 0.01 us -> 35.2 us  [per_device(): lax.all_to_all(states.reshape(devices, OWNER_SLOTS * code_rows, state_dim...]
    pallas_call x0 -> x2, Pallas kernels: none -> 21 us  [the longest x1 11 us: per_device(): pl.pallas_call(relay_kernel, grid=(blocks,), in_specs=[code_spec, pl.Bloc...]
    pallas_call x1, Pallas kernels: 17.1 us -> 24.1 us  [per_device(): pl.pallas_call(functools.partial(state_kernel, docs, device_heads), grid_...]
    unnamed x22 -> x35, local copies, waits for them, and re-layouts: 3.63 us -> 8.76 us
    slice x7 -> x1, local copies, waits for them, and re-layouts: 4.7 us -> 0.17 us  [the longest x1 0.85 us: per_device(): conv_weight[:, :inner_dim]]
    pallas_call x1, Pallas kernels: 9.94 us -> 13.9 us  [per_device(): pl.pallas_call(functools.partial(conv_kernel, groups, state_dim), grid=(b...]
  transfers between devices with their start and end apart: 6 -> 6, of which waited for: 3 -> 5; matrix products, arithmetic and copies ran while one was open for 5% -> 4% of each run, Pallas kernels for 8% -> 15%
where the time goes in v1:
time: 245 us; the launch traced here: 244 us
  waiting for transfers between devices  124 us (51%)
  Pallas kernels  71.9 us (29%)
  starting transfers between devices  23.3 us (10%)
  local copies, waits for them, and re-layouts  17.1 us (7%)
  other arithmetic  6.07 us (2%)
    ppermute x3, waiting for transfers between devices, shifted(): return lax.ppermute(array, axis, pairs)  88.2 us
    all_to_all x1, waiting for transfers between devices, per_device(): lax.all_to_all(states.reshape(devices, OWNER_SLOTS * code_rows, state_dim...  35.2 us
    pallas_call x1, Pallas kernels, per_device(): pl.pallas_call(functools.partial(state_kernel, docs, device_heads), grid_...  24.1 us
    pallas_call x1, Pallas kernels, per_device(): pl.pallas_call(functools.partial(conv_kernel, groups, state_dim), grid=(b...  13.9 us
    pallas_call x1, Pallas kernels, per_device(): pl.pallas_call(main_kernel, grid=(groups,), in_specs=[pl.BlockSpec((group...  12.9 us
    pallas_call x1, Pallas kernels, per_device(): pl.pallas_call(relay_kernel, grid=(blocks,), in_specs=[code_spec, pl.Bloc...  11 us
    pallas_call x1, Pallas kernels, per_device(): pl.pallas_call(deliver_kernel, grid=(devices,), in_specs=[pl.BlockSpec((1...  10 us
    unnamed x35, local copies, waits for them, and re-layouts  8.76 us
  transfers between devices with their start and end apart: 6, of which 5 were waited for; matrix products, arithmetic and copies ran while one was open for 4% of the time, Pallas kernels for 15%

profile of v1, /device:TPU:18, one launch (start us, length us, event | category | flops | bytes accessed | tf_op | source)
XLA Modules:
  0.0 243.7 jit_solution(13388730866429408269)
XLA Ops:
  0.6 4.1 %copy.34 = bf16[256,4096]{0,1:T(8,128)(2,1)} copy(bf16[256,4096]{1,0:T(8,128)(2,1)} %x_ref.1) | data formatting | bytes 4194304 | tf_op args[0]
  4.7 2.9 %copy.36 = bf16[256,16,256]{2,0,1:T(8,128)(2,1)S(1)} copy(bf16[256,16,256]{0,2,1:T(8,128)(2,1)} %bitcast.52) | data formatting | bytes 4194304 | tf_op jit(solution)/shard_map/reshape | solution.py:221
  7.7 0.2 broadcast_in_dim.110
  7.9 2.1 maximum_bitcast_fusion
  10.0 6.3 %all-to-all-start = ((bf16[16,256,384]{2,1,0:T(8,128)(2,1)}), bf16[16,256,384]{2,1,0:T(8,128)(2,1)}, u32[]{:S(2)}, u32[]{:S(2)}) async-start(bf16[16,256,384]{2,1,0:T(8,128)(2,1)} %maximum_bitcast_fusion), calls=%async_computation | async-start | bytes 6291456 | tf_op jit(solution)/shard_map/all_to_all | solution.py:223
  16.4 2.1 collective-permute-start
  18.6 0.6 slice.30
  19.3 0.6 reduce-window.6
  20.8 0.7 iota_compare_fusion.2
  22.0 65.4 %collective-permute-done.rim_x_ref.rim_bc_ref = bf16[8,5120]{1,0:T(8,128)(2,1)S(1)} collective-permute-done((bf16[8,5120]{1,0:T(8,128)(2,1)S(1)}, bf16[8,5120]{1,0:T(8,128)(2,1)S(1)}, u32[]{:S(2)}, u32[]{:S(2)}) %collective-permute-start) | collective-permute-done | bytes 81952 | tf_op jit(solution)/shard_map/ppermute | solution.py:24
  87.4 13.9 %conv.1 = (bf16[16,256,384]{2,1,0:T(8,128)(2,1)}, bf16[256,512]{1,0:T(8,128)(2,1)S(1)}, f32[16,256,128]{2,1,0:T(8,128)S(1)}, s16[16,272,128]{2,1,0:T(8,128)(2,1)S(1)}) custom-call(bf16[256,4096]{1,0:T(8,128)(2,1)} %x_ref.1, bf16[256,1024]{1,0:T(8,128)(2,1)S(1)} %copy-done.2, bf16[8,5120]{1,0:T(8,128)(2,1)S(1)} %collective-permute-done.rim_x_ref.rim_bc_ref, ...), custom_call_target="tpu_custom_call" | custom-call | tf_op jit(solution)/shard_map/conv/pallas_call | solution.py:265
  101.3 1.3 copy-done
  102.6 0.7 copy-done.6
  103.3 2.0 collective-permute-start.1
  105.5 3.5 %broadcast_in_dim.119.factor_ref = f32[16,256,1]{2,1,0:T(8,128)} reshape(f32[16,4,64]{2,1,0:T(4,128)S(1)} %broadcast_in_dim.113) | data formatting | bytes 32768 | tf_op jit(solution)/shard_map/broadcast_in_dim | solution.py:308
  109.6 0.7 pad_maximum_fusion
  110.5 10.7 %collective-permute-done.1.code_ref = s16[16,272,128]{2,1,0:T(8,128)(2,1)S(1)} collective-permute-done((s16[16,272,128]{2,1,0:T(8,128)(2,1)S(1)}, s16[16,272,128]{2,1,0:T(8,128)(2,1)S(1)}, u32[]{:S(2)}, u32[]{:S(2)}) %collective-permute-start.1) | collective-permute-done | bytes 1114144 | tf_op jit(solution)/shard_map/ppermute | solution.py:24
  121.1 1.0 copy-done.11
  122.2 11.0 %relay.1 = s16[16,272,128]{2,1,0:T(8,128)(2,1)} custom-call(s16[16,272,128]{2,1,0:T(8,128)(2,1)} %copy-done.11, f32[16,256,128]{2,1,0:T(8,128)} %copy-done, f32[16,256,1]{2,1,0:T(8,128)} %broadcast_in_dim.119.factor_ref), custom_call_target="tpu_custom_call" | custom-call | tf_op jit(solution)/shard_map/relay/pallas_call | solution.py:311
  133.1 1.9 collective-permute-start.2
  135.0 0.6 fusion.mask_ref
  135.7 5.4 %all-to-all-start.1 = ((f32[16,8,256]{2,1,0:T(8,128)}), f32[16,8,256]{2,1,0:T(8,128)S(1)}, u32[]{:S(2)}, u32[]{:S(2)}) async-start(f32[16,8,256]{2,1,0:T(8,128)} %pad_maximum_fusion), calls=%async_computation.1 | async-start | bytes 262144 | tf_op jit(solution)/shard_map/all_to_all | solution.py:257
  141.1 12.1 %collective-permute-done.2.in_ref = s16[16,272,128]{2,1,0:T(8,128)(2,1)S(1)} collective-permute-done((s16[16,272,128]{2,1,0:T(8,128)(2,1)}, s16[16,272,128]{2,1,0:T(8,128)(2,1)S(1)}, u32[]{:S(2)}, u32[]{:S(2)}) %collective-permute-start.2) | collective-permute-done | bytes 1114144 | tf_op jit(solution)/shard_map/ppermute | solution.py:24
  153.2 0.3 all-to-all-done.1.cd_ref
  153.5 24.1 %doc_states.1 = s16[32,272,128]{2,1,0:T(8,128)(2,1)} custom-call(s32[19]{0:T(128)S(1)} %copy-done.4, s32[18]{0:T(128)S(1)} %multiply_add_fusion.dest_ref, bf16[16,256,384]{2,1,0:T(8,128)(2,1)} %all-to-all-done.recv_ref, f32[16,8,256]{2,1,0:T(8,128)S(1)} %all-to-all-done.1.cd_ref, f32[4096,4]{1,0:T(8,128)S(1)} %fusion.mask_ref, ...), custom_call_target="tpu_custom_call" | custom-call | tf_op jit(solution)/shard_map/doc_states/pallas_call | solution.py:343
  177.6 5.5 %all-to-all-start.2 = ((s16[16,544,128]{2,1,0:T(8,128)(2,1)}), s16[16,544,128]{2,1,0:T(8,128)(2,1)}, u32[]{:S(2)}, u32[]{:S(2)}) async-start(s16[16,544,128]{2,1,0:T(8,128)(2,1)} %bitcast.14), calls=%async_computation.2 | async-start | bytes 4456448 | tf_op jit(solution)/shard_map/all_to_all | solution.py:365
  183.3 0.2 copy.33
  183.5 0.2 copy.32
  184.0 1.6 copy-done.5
  185.6 12.9 %scan_gate_norm.1 = bf16[256,4096]{1,0:T(8,128)(2,1)} custom-call(bf16[16,256,384]{2,1,0:T(8,128)(2,1)} %get-tuple-element.8.send_ref, bf16[256,512]{1,0:T(8,128)(2,1)S(1)} %copy-done.7, f32[64,256]{1,0:T(8,128)S(1)} %copy_bitcast_fusion.1.cum_row_ref, f32[4,256,16]{2,1,0:T(8,128)S(1)} %bitcast.45, f32[4,256,16]{2,1,0:T(8,128)S(1)} %bitcast.44, ...), custom_call_target="tpu_custom_call" | custom-call | flops 3000000000 | bytes 12000000 | tf_op jit(solution)/shard_map/scan_gate_norm/pallas_call | solution.py:383
  198.5 35.2 %all-to-all-done.2 = s16[16,544,128]{2,1,0:T(8,128)(2,1)} async-done(((s16[16,544,128]{2,1,0:T(8,128)(2,1)}), s16[16,544,128]{2,1,0:T(8,128)(2,1)}, u32[]{:S(2)}, u32[]{:S(2)}) %all-to-all-start.2) | async-done | bytes 2228256 | tf_op jit(solution)/shard_map/all_to_all | solution.py:365
  233.7 10.0 %deliver.1 = f32[2,64,64,128]{3,2,1,0:T(8,128)} custom-call(s16[16,2,272,128]{3,2,1,0:T(8,128)(2,1)} %bitcast.15.code_ref), custom_call_target="tpu_custom_call" | custom-call | tf_op jit(solution)/shard_map/deliver/pallas_call | solution.py:368
  (68 shorter events, 2.4 us)
Async XLA Ops:
  4.7 2.9 %copy-start.2 = (bf16[256,1024]{1,0:T(8,128)(2,1)S(1)}, bf16[256,1024]{1,0:T(8,128)(2,1)}, u32[]{:S(2)}) copy-start(bf16[256,1024]{1,0:T(8,128)(2,1)} %bc_ref.1) | copy-start | bytes 1572868
  9.9 6.4 %slice-start = ((bf16[256,1024]{1,0:T(8,128)(2,1)}), bf16[8,1024]{1,0:T(8,128)(2,1)S(1)}, s32[]{:S(2)}) async-start(bf16[256,1024]{1,0:T(8,128)(2,1)} %bc_ref.1), calls=%async_computation.3 | async-start | bytes 32768 | tf_op jit(solution)/shard_map/slice | solution.py:225
  9.9 6.4 %slice-start.1 = ((bf16[256,4096]{1,0:T(8,128)(2,1)}), bf16[8,4096]{1,0:T(8,128)(2,1)S(1)}, s32[]{:S(2)}) async-start(bf16[256,4096]{1,0:T(8,128)(2,1)} %x_ref.1), calls=%async_computation.4 | async-start | bytes 131072 | tf_op jit(solution)/shard_map/slice | solution.py:225
  10.0 8.5 %copy-start.4 = (s32[19]{0:T(128)S(1)}, s32[19]{0:T(128)}, u32[]{:S(2)}) copy-start(s32[19]{0:T(128)} %offsets_ref.1) | copy-start | bytes 232
  10.0 9.2 %copy-start.15 = (f32[64]{0:T(128)S(1)}, f32[64]{0:T(128)}, u32[]{:S(2)}) copy-start(f32[64]{0:T(128)} %param.20) | copy-start | bytes 772
  10.0 9.2 %copy-start.12 = (f32[256,64]{0,1:T(8,128)S(1)}, f32[256,64]{0,1:T(8,128)}, u32[]{:S(2)}) copy-start(f32[256,64]{0,1:T(8,128)} %param.15) | copy-start | bytes 196612
  10.0 9.2 %copy-start.13 = (f32[64]{0:T(128)S(1)}, f32[64]{0:T(128)}, u32[]{:S(2)}) copy-start(f32[64]{0:T(128)} %param.21) | copy-start | bytes 772
  10.0 77.4 %copy-start.1 = (f32[4,5120]{1,0:T(4,128)S(1)}, f32[4,5120]{1,0:T(4,128)}, u32[]{:S(2)}) copy-start(f32[4,5120]{1,0:T(4,128)} %wbc_ref.1) | copy-start | bytes 245764
  10.0 77.4 %copy-start.3 = (f32[5120]{0:T(1024)S(1)}, f32[5120]{0:T(1024)}, u32[]{:S(2)}) copy-start(f32[5120]{0:T(1024)} %param.19) | copy-start | bytes 61444
  10.0 125.7 %all-to-all-start = ((bf16[16,256,384]{2,1,0:T(8,128)(2,1)}), bf16[16,256,384]{2,1,0:T(8,128)(2,1)}, u32[]{:S(2)}, u32[]{:S(2)}) async-start(bf16[16,256,384]{2,1,0:T(8,128)(2,1)} %maximum_bitcast_fusion), calls=%async_computation | async-start | bytes 6291456 | tf_op jit(solution)/shard_map/all_to_all | solution.py:223
  16.4 71.0 %collective-permute-start = (bf16[8,5120]{1,0:T(8,128)(2,1)S(1)}, bf16[8,5120]{1,0:T(8,128)(2,1)S(1)}, u32[]{:S(2)}, u32[]{:S(2)}) collective-permute-start(bf16[8,5120]{1,0:T(8,128)(2,1)S(1)} %pad_maximum_fusion.1), channel_id=1, source_target_pairs={{0,1},{1,2},{2,3},{3,4},{4,5},{5,6},{6,7},{7,8},{8,9},{9,10},{10,1... | collective-permute-start | bytes 245768 | tf_op jit(solution)/shard_map/ppermute | solution.py:24
  19.9 89.1 %copy-start.9 = (f32[64,2,128]{2,0,1:T(8,128)}, f32[64,2,128]{2,0,1:T(8,128)S(1)}, u32[]{:S(2)}) copy-start(f32[64,2,128]{2,0,1:T(8,128)S(1)} %reduce-window.6) | copy-start | bytes 196612
  101.3 1.3 copy-start
  102.6 0.7 copy-start.6
  103.3 6.1 %copy-start.16 = (s32[18]{0:T(128)S(1)}, s32[18]{0:T(128)}, u32[]{:S(2)}) copy-start(s32[18]{0:T(128)} %param.17) | copy-start | bytes 220
  103.3 17.8 %collective-permute-start.1 = (s16[16,272,128]{2,1,0:T(8,128)(2,1)S(1)}, s16[16,272,128]{2,1,0:T(8,128)(2,1)S(1)}, u32[]{:S(2)}, u32[]{:S(2)}) collective-permute-start(s16[16,272,128]{2,1,0:T(8,128)(2,1)S(1)} %get-tuple-element.10), channel_id=1, source_target_pairs={{0,1},{1,2},{2,3},{3,4},{4,5},{5,6},{6,7},{7,8},{8,9},{9,10},{10,1... | collective-permute-start | bytes 3342344 | tf_op jit(solution)/shard_map/ppermute | solution.py:24
  121.1 1.0 copy-start.11
  133.1 20.0 %collective-permute-start.2 = (s16[16,272,128]{2,1,0:T(8,128)(2,1)}, s16[16,272,128]{2,1,0:T(8,128)(2,1)S(1)}, u32[]{:S(2)}, u32[]{:S(2)}) collective-permute-start(s16[16,272,128]{2,1,0:T(8,128)(2,1)} %relay.1), channel_id=1, source_target_pairs={{0,1},{1,2},{2,3},{3,4},{4,5},{5,6},{6,7},{7,8},{8,9},{9,10},{10,1... | collective-permute-start | bytes 3342344 | tf_op jit(solution)/shard_map/ppermute | solution.py:24
  135.7 17.8 %all-to-all-start.1 = ((f32[16,8,256]{2,1,0:T(8,128)}), f32[16,8,256]{2,1,0:T(8,128)S(1)}, u32[]{:S(2)}, u32[]{:S(2)}) async-start(f32[16,8,256]{2,1,0:T(8,128)} %pad_maximum_fusion), calls=%async_computation.1 | async-start | bytes 262144 | tf_op jit(solution)/shard_map/all_to_all | solution.py:257
  177.6 5.5 %copy-start.10 = (f32[64,2,128]{2,0,1:T(8,128)S(1)}, f32[64,2,128]{2,0,1:T(8,128)}, u32[]{:S(2)}) copy-start(f32[64,2,128]{2,0,1:T(8,128)} %copy-done.9) | copy-start | bytes 196612
  177.6 6.2 %copy-start.14 = (f32[64]{0:T(128)S(1)}, f32[64]{0:T(128)}, u32[]{:S(2)}) copy-start(f32[64]{0:T(128)} %param.22) | copy-start | bytes 772
  177.6 6.4 %copy-start.7 = (bf16[256,512]{1,0:T(8,128)(2,1)S(1)}, bf16[256,512]{1,0:T(8,128)(2,1)}, u32[]{:S(2)}) copy-start(bf16[256,512]{1,0:T(8,128)(2,1)} %copy-done.6) | copy-start | bytes 786436
  177.6 6.4 %copy-start.8 = (f32[4096]{0:T(1024)S(1)}, f32[4096]{0:T(1024)}, u32[]{:S(2)}) copy-start(f32[4096]{0:T(1024)} %param.23) | copy-start | bytes 49156
  177.6 56.1 %all-to-all-start.2 = ((s16[16,544,128]{2,1,0:T(8,128)(2,1)}), s16[16,544,128]{2,1,0:T(8,128)(2,1)}, u32[]{:S(2)}, u32[]{:S(2)}) async-start(s16[16,544,128]{2,1,0:T(8,128)(2,1)} %bitcast.14), calls=%async_computation.2 | async-start | bytes 4456448 | tf_op jit(solution)/shard_map/all_to_all | solution.py:365
  184.0 1.6 copy-start.5
